TPU v7x, 256 devices: a whole 4x4x8 slice. The times are simulated.
256 devices in a mesh: pb: 16 (over x, z_hi), sa: 16 (over z_lo, y, core).
Axes of the slice: x: 4, y: 4, z: 8 (z_hi: 4, z_lo: 2; z = z_hi * 2 + z_lo), core: 2. Of those that a mesh axis runs over, the one named last changes fastest.
Arguments:
- question_states: bfloat16 [16, 16, 256, 768], P('pb', 'sa'), may hold values from -16 to 16
- question_ids: int32 [16, 16, 256], P('pb'), may hold values from 0 to 30521, as said below
- q_inner_weight: bfloat16 [768, 3072], P(None, 'sa'), may hold values from -0.21875 to 0.21875
- q_outer_weight: bfloat16 [3072, 768], P('sa'), may hold values from -0.109375 to 0.109375
- q_norm_gain: float32 [768], replicated, may hold values from 0.1 to 1.9
- sql_states: bfloat16 [16, 16, 256, 768], P('sa', 'pb'), may hold values from -16 to 16
- sql_ids: int32 [16, 16, 256], P('sa'), may hold values from 0 to 32099, as said below
- s_inner_weight: bfloat16 [768, 3072], P(None, 'pb'), may hold values from -0.21875 to 0.21875
- s_outer_weight: bfloat16 [3072, 768], P('pb'), may hold values from -0.109375 to 0.109375
- s_norm_gain: float32 [768], replicated, may hold values from 0.1 to 1.9
- positive_column: int32 [256], P('pb'), may hold values from 0 to 255, each once
Outputs:
- loss: float32 [], replicated
- q_inner_grad: float32 [768, 3072], P(None, 'sa')
- q_outer_grad: float32 [3072, 768], P('sa')
- q_gain_grad: float32 [768], replicated
- s_inner_grad: float32 [768, 3072], P(None, 'pb')
- s_outer_grad: float32 [3072, 768], P('pb')
- s_gain_grad: float32 [768], replicated
Inputs may be any that keep to these rules, and one draw needn't show every extreme that they name: `question_ids`: each sequence is a run of nonzero ids followed by padding zeros, the run 3 * 64 long or longer. `sql_ids`: each sequence is a run of nonzero ids followed by padding zeros, the run 3 * 64 long or longer.
All inputs are finite; a program needn't handle non-finite values.
Results may differ from a plain program's by a relative error of at most 0.0051.
Values may be sent and summed in bfloat16 or wider, within the bound.
A program may use at most 128 MiB of HBM per device.

v0:
```python
import math
import jax
import jax.numpy as jnp
from jax import lax
from jax.sharding import PartitionSpec as P

D = 768
HIGH = lax.Precision.HIGHEST


def apply_rms_norm(input_float, norm_gain_vector, root_mean_square):
    if root_mean_square:
        input_normalized = input_float * lax.rsqrt(
            jnp.mean(input_float * input_float, axis=-1, keepdims=True) + 1e-06
        )
    else:
        mean_removed = input_float - jnp.mean(input_float, axis=-1, keepdims=True)
        input_normalized = mean_removed * lax.rsqrt(
            jnp.mean(mean_removed * mean_removed, axis=-1, keepdims=True) + 1e-05
        )
    return (input_normalized, (input_normalized * norm_gain_vector).astype(jnp.bfloat16))


def gelu_value(v):
    return 0.5 * v * (1.0 + lax.erf(v / math.sqrt(2.0)))


def gelu_slope(v):
    return 0.5 * (1.0 + lax.erf(v / math.sqrt(2.0))) + v * jnp.exp(-0.5 * v * v) / math.sqrt(
        2.0 * math.pi
    )


def pool_weights(ids):
    mask = (ids > 0).astype(jnp.float32)
    return mask / jnp.sum(mask, axis=-1, keepdims=True)


def forward_block(states, ids, inner, norm_gain_vector, root_mean_square):
    count, length, width = states.shape
    input_float = states.astype(jnp.float32).reshape(count * length, width)
    input_normalized, normalized_rows = apply_rms_norm(
        input_float, norm_gain_vector, root_mean_square
    )
    pre = jnp.dot(normalized_rows, inner, preferred_element_type=jnp.float32)
    hidden = gelu_value(pre).reshape(count, length, -1)
    return jnp.einsum("nt,ntf->nf", pool_weights(ids), hidden, precision=HIGH)


def residual_pool(states, ids):
    return jnp.einsum("nt,ntd->nd", pool_weights(ids), states.astype(jnp.float32), precision=HIGH)


def backward_block(states, ids, inner, norm_gain_vector, root_mean_square, hidden_grad):
    count, length, width = states.shape
    input_float = states.astype(jnp.float32).reshape(count * length, width)
    input_normalized, normalized_rows = apply_rms_norm(
        input_float, norm_gain_vector, root_mean_square
    )
    pre = jnp.dot(normalized_rows, inner, preferred_element_type=jnp.float32)
    weights = pool_weights(ids)
    slope = gelu_slope(pre).reshape(count, length, -1)
    dpre = (
        (weights[:, :, None] * hidden_grad[:, None, :] * slope)
        .reshape(count * length, -1)
        .astype(jnp.bfloat16)
    )
    inner_layer_grad = lax.dot_general(
        normalized_rows, dpre, (((0,), (0,)), ((), ())), preferred_element_type=jnp.float32
    )
    normalized_grad = lax.dot_general(
        dpre, inner, (((1,), (1,)), ((), ())), preferred_element_type=jnp.float32
    )
    return (inner_layer_grad, jnp.sum(input_normalized * normalized_grad, axis=0))


def per_device(
    question_states,
    question_ids,
    q_inner_weight,
    q_outer_weight,
    q_norm_gain,
    sql_states,
    sql_ids,
    s_inner_weight,
    s_outer_weight,
    s_norm_gain,
    positive_column,
):
    scale = 1.0 / math.sqrt(D)
    q_table = question_ids[0]
    s_table = sql_ids[0]
    q_rows = q_table.shape[0]
    s_rows = s_table.shape[0]
    own_count = question_states.shape[1]
    q_place = lax.axis_index("sa")
    s_place = lax.axis_index("pb")

    def s_forward(piece):
        pooled = forward_block(piece[0], s_table, s_inner_weight, s_norm_gain, True)
        return pooled

    ids = q_table
    pooled = forward_block(
        lax.all_gather(question_states, "sa", axis=1, tiled=True)[0],
        ids,
        q_inner_weight,
        q_norm_gain,
        False,
    )
    s_pooled = s_forward(lax.all_gather(sql_states, "pb", axis=1, tiled=True))
    q_first = q_place * own_count
    s_first = s_place * own_count
    q_own = residual_pool(
        question_states[0], lax.dynamic_slice_in_dim(q_table, q_first, own_count, 0)
    )
    s_own = residual_pool(sql_states[0], lax.dynamic_slice_in_dim(s_table, s_first, own_count, 0))
    q_resid = lax.dynamic_update_slice_in_dim(
        jnp.zeros((q_rows, D), jnp.float32), q_own, q_first, 0
    )
    s_resid = lax.dynamic_update_slice_in_dim(
        jnp.zeros((s_rows, D), jnp.float32), s_own, s_first, 0
    )
    q_outer_f = q_outer_weight.astype(jnp.float32)
    s_outer_f = s_outer_weight.astype(jnp.float32)
    q_embed = lax.psum(jnp.dot(pooled, q_outer_f, precision=HIGH) + q_resid, "sa")
    s_embed = lax.psum(jnp.dot(s_pooled, s_outer_f, precision=HIGH) + s_resid, "pb")
    tile = scale * lax.dot_general(q_embed, s_embed, (((1,), (1,)), ((), ())), precision=HIGH)
    columns = q_place * s_rows + jnp.arange(s_rows, dtype=jnp.int32)
    match = (positive_column[:, None] == columns[None, :]).astype(jnp.float32)
    row_top = lax.pmax(jnp.max(tile, axis=1), "sa")
    row_total, row_pos = lax.psum(
        (jnp.sum(jnp.exp(tile - row_top[:, None]), axis=1), jnp.sum(match * tile, axis=1)), "sa"
    )
    col_top = lax.pmax(jnp.max(tile, axis=0), "pb")
    col_total, col_pos = lax.psum(
        (jnp.sum(jnp.exp(tile - col_top[None, :]), axis=0), jnp.sum(match * tile, axis=0)), "pb"
    )
    row_lse = row_top + jnp.log(row_total)
    col_lse = col_top + jnp.log(col_total)
    pairs = q_rows * lax.axis_size("pb")
    row_part = jnp.where(q_place == 0, jnp.sum(row_lse - row_pos), 0.0)
    col_part = jnp.where(s_place == 0, jnp.sum(col_lse - col_pos), 0.0)
    loss_part = (row_part + col_part) / (2.0 * pairs)
    dscore = 0.5 * (
        jnp.exp(tile - row_lse[:, None]) + jnp.exp(tile - col_lse[None, :]) - 2.0 * match
    )
    q_grad = lax.psum(scale * jnp.dot(dscore, s_embed, precision=HIGH), "sa")
    s_grad = lax.psum(
        scale * lax.dot_general(dscore, q_embed, (((0,), (0,)), ((), ())), precision=HIGH), "pb"
    )
    q_outer_part = lax.dot_general(pooled, q_grad, (((0,), (0,)), ((), ())), precision=HIGH)
    s_outer_part = lax.dot_general(s_pooled, s_grad, (((0,), (0,)), ((), ())), precision=HIGH)
    q_hidden_grad = lax.dot_general(q_grad, q_outer_f, (((1,), (1,)), ((), ())), precision=HIGH)
    s_hidden_grad = lax.dot_general(s_grad, s_outer_f, (((1,), (1,)), ((), ())), precision=HIGH)

    def s_backward(piece):
        inner_layer_grad, gain_grad = backward_block(
            piece[0], s_table, s_inner_weight, s_norm_gain, True, s_hidden_grad
        )
        return (inner_layer_grad, gain_grad)

    ids = q_table
    inner_layer_grad, gain_grad = backward_block(
        lax.all_gather(question_states, "sa", axis=1, tiled=True)[0],
        ids,
        q_inner_weight,
        q_norm_gain,
        False,
        q_hidden_grad,
    )
    s_inner_part, s_gain_part = s_backward(lax.all_gather(sql_states, "pb", axis=1, tiled=True))
    q_inner_grad, q_outer_grad = lax.psum((inner_layer_grad, q_outer_part), "pb")
    s_inner_grad, s_outer_grad = lax.psum((s_inner_part, s_outer_part), "sa")
    q_gain_grad, s_gain_grad, loss = lax.psum((gain_grad, s_gain_part, loss_part), ("pb", "sa"))
    return (loss, q_inner_grad, q_outer_grad, q_gain_grad, s_inner_grad, s_outer_grad, s_gain_grad)


def solution(mesh):
    placed = (
        P("pb", "sa", None, None),
        P("pb", None, None),
        P(None, "sa"),
        P("sa", None),
        P(),
        P("sa", "pb", None, None),
        P("sa", None, None),
        P(None, "pb"),
        P("pb", None),
        P(),
        P("pb"),
    )
    return jax.shard_map(
        per_device,
        mesh=mesh,
        in_specs=placed,
        out_specs=(P(), P(None, "sa"), P("sa", None), P(), P(None, "pb"), P("pb", None), P()),
        check_vma=False,
    )
```

profile of v0, /device:TPU:1, one launch (start us, length us, event | category | flops | bytes accessed | tf_op | source)
XLA Modules:
  0.0 849.9 jit_solution(1982385561405561287)
XLA Ops:
  15.7 43.4 %all-gather.3.cloned.1.call-done = bf16[1,16,256,768]{3,2,0,1:T(8,128)(2,1)} async-done(((bf16[1,1,256,768]{3,2,0,1:T(8,128)(2,1)}), bf16[1,16,256,768]{3,2,0,1:T(8,128)(2,1)}) %all-gather.3.cloned.1.call-update) | async-done | bytes 6291472 | tf_op jit(solution)/shard_map/all_gather | solution.py:105
  59.1 3.8 convert_reduce_fusion
  63.7 1.9 multiply_reduce_fusion.3
  65.7 2.2 multiply_convert_fusion.1
  67.9 2.5 multiply_multiply_fusion.3
  70.5 2.7 fusion.16
  74.9 56.9 %psum.105 = f32[16,768]{1,0:T(8,128)S(1)} all-reduce(f32[16,768]{1,0:T(8,128)S(1)} %add.105), channel_id=1, replica_groups=mesh['pb'=16,'sa'=16] {'sa'}, use_global_device_ids=true, to_apply=%region_4.0 | all-reduce | flops 12288 | bytes 98304 | tf_op jit(solution)/shard_map/psum | solution.py:126
  131.7 27.8 %all-gather.5.cloned.1.call-done = bf16[1,16,256,768]{3,2,0,1:T(8,128)(2,1)} async-done(((bf16[1,1,256,768]{3,2,0,1:T(8,128)(2,1)}), bf16[1,16,256,768]{3,2,0,1:T(8,128)(2,1)}) %all-gather.5.cloned.1.call-update) | async-done | bytes 6291472 | tf_op jit(solution)/shard_map/all_gather | solution.py:111
  159.5 4.2 multiply_reduce_fusion.2
  165.9 3.6 multiply_multiply_fusion.2
  169.6 2.7 fusion.13
  174.8 67.6 %psum.106 = f32[16,768]{1,0:T(8,128)} all-reduce(f32[16,768]{1,0:T(8,128)S(1)} %add.109), channel_id=1, replica_groups=mesh['pb'=16,'sa'=16] {'pb'}, use_global_device_ids=true, to_apply=%region_8.0 | all-reduce | flops 12288 | bytes 98304 | tf_op jit(solution)/shard_map/psum | solution.py:127
  243.6 41.3 %pmax.14 = f32[16]{0:T(128)S(1)} all-reduce(f32[16]{0:T(128)S(1)} %get-tuple-element.12), channel_id=1, replica_groups=mesh['pb'=16,'sa'=16] {'sa'}, use_global_device_ids=true, to_apply=%region_10.0 | all-reduce | flops 16 | bytes 128 | tf_op jit(solution)/shard_map/pmax | solution.py:131
  284.9 32.1 %pmax.15 = f32[16]{0:T(128)S(1)} all-reduce(f32[16]{0:T(128)S(1)} %get-tuple-element.11), channel_id=1, replica_groups=mesh['pb'=16,'sa'=16] {'pb'}, use_global_device_ids=true, to_apply=%region_17.0 | all-reduce | flops 16 | bytes 128 | tf_op jit(solution)/shard_map/pmax | solution.py:135
  318.3 34.1 %psum.107 = f32[16]{0:T(128)S(1)} all-reduce(f32[16]{0:T(128)S(1)} %get-tuple-element.10), channel_id=1, replica_groups=mesh['pb'=16,'sa'=16] {'sa'}, use_global_device_ids=true, to_apply=%region_12.0 | all-reduce | flops 16 | bytes 128 | tf_op jit(solution)/shard_map/psum | solution.py:132
  352.4 34.7 %psum.109 = f32[16]{0:T(128)S(1)} all-reduce(f32[16]{0:T(128)S(1)} %get-tuple-element.9), channel_id=1, replica_groups=mesh['pb'=16,'sa'=16] {'pb'}, use_global_device_ids=true, to_apply=%region_19.0 | all-reduce | flops 16 | bytes 128 | tf_op jit(solution)/shard_map/psum | solution.py:136
  390.5 56.9 %all-reduce.1 = (f32[16]{0:T(128)}, f32[16,768]{1,0:T(8,128)S(1)}) all-reduce(f32[16]{0:T(128)} %get-tuple-element.8, f32[16,768]{1,0:T(8,128)} %convolution_multiply_fusion.1), channel_id=1, replica_groups=mesh['pb'=16,'sa'=16] {'sa'}, use_global_device_ids=true, to_apply=%region_14.0 | all-reduce | flops 12304 | bytes 98432 | tf_op jit(solution)/shard_map/psum | solution.py:132
  448.7 2.2 fusion.29
  451.4 4.4 copy.39
  455.8 63.2 %all-reduce.3 = (f32[16]{0:T(128)}, f32[16,768]{1,0:T(8,128)S(1)}) all-reduce(f32[16]{0:T(128)} %get-tuple-element.7, f32[16,768]{1,0:T(8,128)S(1)} %copy-done.27), channel_id=1, replica_groups=mesh['pb'=16,'sa'=16] {'pb'}, use_global_device_ids=true, to_apply=%region_21.0 | all-reduce | flops 12304 | bytes 98432 | tf_op jit(solution)/shard_map/psum | solution.py:136
  520.8 4.5 copy.42
  527.9 2.2 fusion.65
  530.3 2.8 fusion.12
  534.6 5.0 fusion.66
  539.8 5.9 multiply_reduce_fusion
  548.2 4.8 multiply_reduce_fusion.1
  553.1 89.9 %all-reduce = (f32[]{:T(128)}, f32[768]{0:T(1024)}, f32[768]{0:T(1024)}) all-reduce(f32[]{:T(128)S(6)} %div.107, f32[768]{0:T(1024)S(1)} %multiply_reduce_fusion.1, f32[768]{0:T(1024)S(1)} %multiply_reduce_fusion), channel_id=1, replica_groups=mesh['pb'=16,'sa'=16] {'pb','sa'}, use_global_device_ids=true, to_apply=%region_23.24 | all-reduce | flops 1537 | bytes 12296 | tf_op jit(solution)/shard_map/psum | solution.py:175
  643.0 57.8 %all-reduce.10.cloned.1.call-done = (f32[768,192]{0,1:T(8,128)}, f32[192,768]{1,0:T(8,128)}) async-done(((f32[768,192]{0,1:T(8,128)}, f32[192,768]{1,0:T(8,128)}), (f32[768,192]{0,1:T(8,128)}, f32[192,768]{1,0:T(8,128)})) %all-reduce.10.cloned.1.call-update) | async-done | bytes 1179664 | tf_op jit(solution)/shard_map/psum | solution.py:173
  700.8 135.9 %all-reduce.8.cloned.1.call-done = (f32[768,192]{0,1:T(8,128)}, f32[192,768]{1,0:T(8,128)}) async-done(((f32[768,192]{0,1:T(8,128)}, f32[192,768]{1,0:T(8,128)}), (f32[768,192]{0,1:T(8,128)}, f32[192,768]{1,0:T(8,128)})) %all-reduce.8.cloned.1.call-update) | async-done | bytes 1179664 | tf_op jit(solution)/shard_map/psum | solution.py:174
  836.7 2.0 copy.77
  838.7 1.9 copy.78
  840.6 1.9 copy.79
  (127 shorter events, 30.0 us)
Async XLA Ops:
  7.2 158.7 %copy-start = (bf16[768,192]{0,1:T(8,128)(2,1)S(1)}, bf16[768,192]{0,1:T(8,128)(2,1)}, u32[]{:S(2)}) copy-start(bf16[768,192]{0,1:T(8,128)(2,1)} %param.18) | copy-start | bytes 884740
  7.2 51.9 %all-gather.3.cloned.1.call-start = ((), (), s32[]{:S(2)}) async-start(), calls=%async_computation | async-start | bytes 6684672 | tf_op jit(solution)/shard_map/all_gather | solution.py:105
  7.9 151.6 %all-gather.5.cloned.1.call-start = ((), (), s32[]{:S(2)}) async-start(), calls=%async_computation.1 | async-start | bytes 6684672 | tf_op jit(solution)/shard_map/all_gather | solution.py:111
  8.7 692.1 %all-reduce.10.cloned.1.call-start = ((), (), s32[]{:S(2)}) async-start(), calls=%async_computation.3 | async-start | bytes 2359296 | tf_op jit(solution)/shard_map/psum | solution.py:173
  59.1 4.6 copy-start.1
  67.9 2.6 copy-start.2
  70.5 2.7 copy-start.12
  70.5 3.3 copy-start.7
  131.7 32.7 %copy-start.29 = (f32[768]{0:T(1024)S(1)}, f32[768]{0:T(1024)}, u32[]{:S(2)}) copy-start(f32[768]{0:T(1024)} %param.20) | copy-start | bytes 9220
  159.5 4.9 copy-start.4
  165.9 3.7 copy-start.3
  165.9 3.7 copy-start.20
  169.6 2.7 copy-start.13
  169.6 2.9 copy-start.8
  352.4 38.1 %copy-start.34 = (f32[16]{0:T(128)}, f32[16]{0:T(128)S(1)}, u32[]{:S(2)}) copy-start(f32[16]{0:T(128)S(1)} %log_add_fusion.1) | copy-start | bytes 196
  387.1 3.3 copy-start.32
  451.4 4.4 copy-start.27
  520.7 4.6 copy-start.6
  520.7 4.6 copy-start.19
  520.8 7.1 slice-start
  525.3 2.6 slice-start.1
  530.2 306.5 %all-reduce.8.cloned.1.call-start = ((), (), s32[]{:S(2)}) async-start(), calls=%async_computation.2 | async-start | bytes 2359296 | tf_op jit(solution)/shard_map/psum | solution.py:174
  534.6 5.1 copy-start.26
  539.7 6.0 copy-start.30
  539.7 6.0 copy-start.35
  539.7 7.2 copy-start.31
  539.7 7.2 copy-start.33
  539.7 8.5 copy-start.10
  539.7 8.5 copy-start.16
  539.7 8.5 copy-start.22
  539.7 8.5 copy-start.24
  836.7 5.8 copy-start.14
  (10 other events, 17.2 us)
Sparse Core Ops, SparseCore 0:
  9.9 49.1 all-gather.2
  61.5 97.9 all-gather.4
  530.3 170.4 all-reduce.9
  703.9 132.7 all-reduce.7
where the time goes:
time: 851 us; the launch traced here: 850 us
  blocking collectives  477 us (56%)
  waiting for transfers between devices  266 us (31%)
  matrix products  43.3 us (5%)
  other arithmetic  26 us (3%)
  local copies, waits for them, and re-layouts  20.5 us (2%)
  between operations  17 us (2%)
    psum x1, waiting for transfers between devices, per_device(): s_inner_grad, s_outer_grad = lax.psum((s_inner_part, s_outer_part), 'sa')  136 us
    psum x2, blocking collectives, per_device(): lax.psum((jnp.sum(jnp.exp(tile - col_top[None, :]), axis=0), jnp.sum(matc...  97.9 us
    psum x2, blocking collectives, per_device(): lax.psum((jnp.sum(jnp.exp(tile - row_top[:, None]), axis=1), jnp.sum(matc...  91 us
    psum x1, blocking collectives, per_device(): lax.psum((gain_grad, s_gain_part, loss_part), ('pb', 'sa'))  89.9 us
    psum x1, blocking collectives, per_device(): lax.psum(jnp.dot(s_pooled, s_outer_f, precision=HIGH) + s_resid, 'pb')  67.6 us
    psum x1, waiting for transfers between devices, per_device(): lax.psum((inner_layer_grad, q_outer_part), 'pb')  57.8 us
    psum x1, blocking collectives, per_device(): lax.psum(jnp.dot(pooled, q_outer_f, precision=HIGH) + q_resid, 'sa')  56.9 us
    all_gather x1, waiting for transfers between devices, per_device(): lax.all_gather(question_states, 'sa', axis=1, tiled=True)[0]  43.4 us
  transfers between devices with their start and end apart: 4, of which 4 were waited for; matrix products, arithmetic and copies ran while one was open for 5% of the time, Pallas kernels for 0%

commit v1 on v0

--- a/solution.py
+++ b/solution.py
@@ -172,7 +172,9 @@
     s_inner_part, s_gain_part = s_backward(lax.all_gather(sql_states, "pb", axis=1, tiled=True))
     q_inner_grad, q_outer_grad = lax.psum((inner_layer_grad, q_outer_part), "pb")
     s_inner_grad, s_outer_grad = lax.psum((s_inner_part, s_outer_part), "sa")
-    q_gain_grad, s_gain_grad, loss = lax.psum((gain_grad, s_gain_part, loss_part), ("pb", "sa"))
+    q_gain_grad, s_gain_grad, loss = lax.psum(
+        lax.psum((gain_grad, s_gain_part, loss_part), "pb"), "sa"
+    )
     return (loss, q_inner_grad, q_outer_grad, q_gain_grad, s_inner_grad, s_outer_grad, s_gain_grad)
 
 

time: 851 us -> 851 us (level)
    psum x1 -> x2, blocking collectives: 89.9 us -> 88.8 us  [the longest x1 53 us: per_device(): lax.psum(lax.psum((gain_grad, s_gain_part, loss_part), 'pb'), 'sa')]
where the time goes in v1:
time: 851 us; the launch traced here: 850 us
  blocking collectives  476 us (56%)
  waiting for transfers between devices  268 us (31%)
  matrix products  43.3 us (5%)
  other arithmetic  26 us (3%)
  local copies, waits for them, and re-layouts  20.5 us (2%)
  between operations  17 us (2%)
    psum x1, waiting for transfers between devices, per_device(): s_inner_grad, s_outer_grad = lax.psum((s_inner_part, s_outer_part), 'sa')  136 us
    psum x2, blocking collectives, per_device(): lax.psum((jnp.sum(jnp.exp(tile - col_top[None, :]), axis=0), jnp.sum(matc...  97.9 us
    psum x2, blocking collectives, per_device(): lax.psum((jnp.sum(jnp.exp(tile - row_top[:, None]), axis=1), jnp.sum(matc...  91 us
    psum x1, blocking collectives, per_device(): lax.psum(jnp.dot(s_pooled, s_outer_f, precision=HIGH) + s_resid, 'pb')  67.6 us
    psum x1, waiting for transfers between devices, per_device(): lax.psum((inner_layer_grad, q_outer_part), 'pb')  59.8 us
    psum x1, blocking collectives, per_device(): lax.psum(jnp.dot(pooled, q_outer_f, precision=HIGH) + q_resid, 'sa')  56.9 us
    psum x1, blocking collectives, per_device(): lax.psum(lax.psum((gain_grad, s_gain_part, loss_part), 'pb'), 'sa')  53 us
    all_gather x1, waiting for transfers between devices, per_device(): lax.all_gather(question_states, 'sa', axis=1, tiled=True)[0]  43.4 us
  transfers between devices with their start and end apart: 4, of which 4 were waited for; matrix products, arithmetic and copies ran while one was open for 5% of the time, Pallas kernels for 0%

profile of v1, /device:TPU:1, one launch (start us, length us, event | category | flops | bytes accessed | tf_op | source)
XLA Modules:
  0.0 850.4 jit_solution(10881665910788480222)
XLA Ops:
  15.7 43.4 %all-gather.3.cloned.1.call-done = bf16[1,16,256,768]{3,2,0,1:T(8,128)(2,1)} async-done(((bf16[1,1,256,768]{3,2,0,1:T(8,128)(2,1)}), bf16[1,16,256,768]{3,2,0,1:T(8,128)(2,1)}) %all-gather.3.cloned.1.call-update) | async-done | bytes 6291472 | tf_op jit(solution)/shard_map/all_gather | solution.py:105
  59.1 3.8 convert_reduce_fusion
  63.7 1.9 multiply_reduce_fusion.3
  65.7 2.2 multiply_convert_fusion.1
  67.9 2.5 multiply_multiply_fusion.3
  70.5 2.7 fusion.16
  74.9 56.9 %psum.126 = f32[16,768]{1,0:T(8,128)S(1)} all-reduce(f32[16,768]{1,0:T(8,128)S(1)} %add.111), channel_id=1, replica_groups=mesh['pb'=16,'sa'=16] {'sa'}, use_global_device_ids=true, to_apply=%region_4.0 | all-reduce | flops 12288 | bytes 98304 | tf_op jit(solution)/shard_map/psum | solution.py:126
  131.7 27.8 %all-gather.5.cloned.1.call-done = bf16[1,16,256,768]{3,2,0,1:T(8,128)(2,1)} async-done(((bf16[1,1,256,768]{3,2,0,1:T(8,128)(2,1)}), bf16[1,16,256,768]{3,2,0,1:T(8,128)(2,1)}) %all-gather.5.cloned.1.call-update) | async-done | bytes 6291472 | tf_op jit(solution)/shard_map/all_gather | solution.py:111
  159.5 4.2 multiply_reduce_fusion.2
  165.9 3.6 multiply_multiply_fusion.2
  169.6 2.7 fusion.13
  174.8 67.6 %psum.127 = f32[16,768]{1,0:T(8,128)} all-reduce(f32[16,768]{1,0:T(8,128)S(1)} %add.115), channel_id=1, replica_groups=mesh['pb'=16,'sa'=16] {'pb'}, use_global_device_ids=true, to_apply=%region_8.0 | all-reduce | flops 12288 | bytes 98304 | tf_op jit(solution)/shard_map/psum | solution.py:127
  243.6 41.3 %pmax.14 = f32[16]{0:T(128)S(1)} all-reduce(f32[16]{0:T(128)S(1)} %get-tuple-element.12), channel_id=1, replica_groups=mesh['pb'=16,'sa'=16] {'sa'}, use_global_device_ids=true, to_apply=%region_10.0 | all-reduce | flops 16 | bytes 128 | tf_op jit(solution)/shard_map/pmax | solution.py:131
  284.9 32.1 %pmax.15 = f32[16]{0:T(128)S(1)} all-reduce(f32[16]{0:T(128)S(1)} %get-tuple-element.11), channel_id=1, replica_groups=mesh['pb'=16,'sa'=16] {'pb'}, use_global_device_ids=true, to_apply=%region_17.0 | all-reduce | flops 16 | bytes 128 | tf_op jit(solution)/shard_map/pmax | solution.py:135
  318.3 34.1 %psum.128 = f32[16]{0:T(128)S(1)} all-reduce(f32[16]{0:T(128)S(1)} %get-tuple-element.10), channel_id=1, replica_groups=mesh['pb'=16,'sa'=16] {'sa'}, use_global_device_ids=true, to_apply=%region_12.0 | all-reduce | flops 16 | bytes 128 | tf_op jit(solution)/shard_map/psum | solution.py:132
  352.4 34.7 %psum.130 = f32[16]{0:T(128)S(1)} all-reduce(f32[16]{0:T(128)S(1)} %get-tuple-element.9), channel_id=1, replica_groups=mesh['pb'=16,'sa'=16] {'pb'}, use_global_device_ids=true, to_apply=%region_19.0 | all-reduce | flops 16 | bytes 128 | tf_op jit(solution)/shard_map/psum | solution.py:136
  390.5 56.9 %all-reduce.1 = (f32[16]{0:T(128)}, f32[16,768]{1,0:T(8,128)S(1)}) all-reduce(f32[16]{0:T(128)} %get-tuple-element.8, f32[16,768]{1,0:T(8,128)} %convolution_multiply_fusion.1), channel_id=1, replica_groups=mesh['pb'=16,'sa'=16] {'sa'}, use_global_device_ids=true, to_apply=%region_14.0 | all-reduce | flops 12304 | bytes 98432 | tf_op jit(solution)/shard_map/psum | solution.py:132
  448.7 2.2 fusion.29
  451.4 4.4 copy.39
  455.8 63.2 %all-reduce.4 = (f32[16]{0:T(128)}, f32[16,768]{1,0:T(8,128)S(1)}) all-reduce(f32[16]{0:T(128)} %get-tuple-element.7, f32[16,768]{1,0:T(8,128)S(1)} %copy-done.27), channel_id=1, replica_groups=mesh['pb'=16,'sa'=16] {'pb'}, use_global_device_ids=true, to_apply=%region_21.0 | all-reduce | flops 12304 | bytes 98432 | tf_op jit(solution)/shard_map/psum | solution.py:136
  520.8 4.5 copy.42
  527.9 2.2 fusion.65
  530.3 2.8 fusion.12
  534.6 5.0 fusion.66
  539.8 5.9 multiply_reduce_fusion
  548.2 4.8 multiply_reduce_fusion.1
  553.1 35.8 %all-reduce.3 = (f32[]{:T(128)}, f32[768]{0:T(1024)S(1)}, f32[768]{0:T(1024)S(1)}) all-reduce(f32[]{:T(128)S(6)} %div.107, f32[768]{0:T(1024)S(1)} %multiply_reduce_fusion.1, f32[768]{0:T(1024)S(1)} %multiply_reduce_fusion), channel_id=1, replica_groups=mesh['pb'=16,'sa'=16] {'pb'}, use_global_device_ids=true, to_apply=%region_23.24 | all-reduce | flops 1537 | bytes 12296 | tf_op jit(solution)/shard_map/psum | solution.py:176
  588.8 53.0 %all-reduce = (f32[]{:T(128)}, f32[768]{0:T(1024)}, f32[768]{0:T(1024)}) all-reduce(f32[]{:T(128)} %get-tuple-element.20, f32[768]{0:T(1024)S(1)} %get-tuple-element.21, f32[768]{0:T(1024)S(1)} %get-tuple-element.22), channel_id=1, replica_groups=mesh['pb'=16,'sa'=16] {'sa'}, use_global_device_ids=true, to_apply=%region_24.25 | all-reduce | flops 1537 | bytes 12296 | tf_op jit(solution)/shard_map/psum | solution.py:175
  641.9 59.8 %all-reduce.11.cloned.1.call-done = (f32[768,192]{0,1:T(8,128)}, f32[192,768]{1,0:T(8,128)}) async-done(((f32[768,192]{0,1:T(8,128)}, f32[192,768]{1,0:T(8,128)}), (f32[768,192]{0,1:T(8,128)}, f32[192,768]{1,0:T(8,128)})) %all-reduce.11.cloned.1.call-update) | async-done | bytes 1179664 | tf_op jit(solution)/shard_map/psum | solution.py:173
  701.7 135.5 %all-reduce.9.cloned.1.call-done = (f32[768,192]{0,1:T(8,128)}, f32[192,768]{1,0:T(8,128)}) async-done(((f32[768,192]{0,1:T(8,128)}, f32[192,768]{1,0:T(8,128)}), (f32[768,192]{0,1:T(8,128)}, f32[192,768]{1,0:T(8,128)})) %all-reduce.9.cloned.1.call-update) | async-done | bytes 1179664 | tf_op jit(solution)/shard_map/psum | solution.py:174
  837.2 2.0 copy.77
  839.2 1.9 copy.78
  (128 shorter events, 31.9 us)
Async XLA Ops:
  7.2 158.7 %copy-start = (bf16[768,192]{0,1:T(8,128)(2,1)S(1)}, bf16[768,192]{0,1:T(8,128)(2,1)}, u32[]{:S(2)}) copy-start(bf16[768,192]{0,1:T(8,128)(2,1)} %param.18) | copy-start | bytes 884740
  7.2 51.9 %all-gather.3.cloned.1.call-start = ((), (), s32[]{:S(2)}) async-start(), calls=%async_computation | async-start | bytes 6684672 | tf_op jit(solution)/shard_map/all_gather | solution.py:105
  7.9 151.6 %all-gather.5.cloned.1.call-start = ((), (), s32[]{:S(2)}) async-start(), calls=%async_computation.1 | async-start | bytes 6684672 | tf_op jit(solution)/shard_map/all_gather | solution.py:111
  8.7 693.0 %all-reduce.11.cloned.1.call-start = ((), (), s32[]{:S(2)}) async-start(), calls=%async_computation.3 | async-start | bytes 2359296 | tf_op jit(solution)/shard_map/psum | solution.py:173
  59.1 4.6 copy-start.1
  67.9 2.6 copy-start.2
  70.5 2.7 copy-start.12
  70.5 3.3 copy-start.7
  131.7 32.7 %copy-start.29 = (f32[768]{0:T(1024)S(1)}, f32[768]{0:T(1024)}, u32[]{:S(2)}) copy-start(f32[768]{0:T(1024)} %param.20) | copy-start | bytes 9220
  159.5 4.9 copy-start.4
  165.9 3.7 copy-start.3
  165.9 3.7 copy-start.20
  169.6 2.7 copy-start.13
  169.6 2.9 copy-start.8
  352.4 38.1 %copy-start.34 = (f32[16]{0:T(128)}, f32[16]{0:T(128)S(1)}, u32[]{:S(2)}) copy-start(f32[16]{0:T(128)S(1)} %log_add_fusion.1) | copy-start | bytes 196
  387.1 3.3 copy-start.32
  451.4 4.4 copy-start.27
  520.7 4.6 copy-start.6
  520.7 4.6 copy-start.19
  520.8 7.1 slice-start
  525.3 2.6 slice-start.1
  530.2 307.0 %all-reduce.9.cloned.1.call-start = ((), (), s32[]{:S(2)}) async-start(), calls=%async_computation.2 | async-start | bytes 2359296 | tf_op jit(solution)/shard_map/psum | solution.py:174
  534.6 5.1 copy-start.26
  539.7 6.0 copy-start.30
  539.7 6.0 copy-start.35
  539.7 7.2 copy-start.31
  539.7 7.2 copy-start.33
  539.7 8.5 copy-start.10
  539.7 8.5 copy-start.16
  539.7 8.5 copy-start.22
  539.7 8.5 copy-start.24
  837.2 5.8 copy-start.14
  (10 other events, 17.2 us)
Sparse Core Ops, SparseCore 0:
  9.9 49.1 all-gather.2
  61.5 97.9 all-gather.4
  530.3 171.2 all-reduce.10
  704.8 132.3 all-reduce.8
